TPU v7x, 256 devices: a whole 4x4x8 slice. The times are simulated.
256 devices in a mesh: frame: 8 (over z_lo, x), brick: 32 (over y, z_hi, core).
Axes of the slice: x: 4, y: 4, z: 8 (z_hi: 4, z_lo: 2; z = z_hi * 2 + z_lo), core: 2. Of those that a mesh axis runs over, the one named last changes fastest.
Arguments:
- intensity: float32 [32, 512, 128], P('frame', 'brick'), may hold values from 0.1 to 10
- correction: float32 [32, 512, 128], P('frame', 'brick'), may hold values from 0.3 to 3
- splitting: bfloat16 [32, 32, 8, 128, 512], P('frame', 'brick'), may hold values from 0 to 0.015625
- block_count: int32 [32, 32], P('frame', 'brick'), may hold values from 1 to 8, 128 in all within a row
- pix_index: int32 [32, 32, 8], P('frame', 'brick'), may hold values from 0 to 511, as said below
- vox_offset: int32 [32, 32, 8], P('frame', 'brick'), may hold values from 0 to 129
Outputs:
- merged: float32 [32, 128, 512], P('brick', 'frame')
- weight: float32 [32, 128, 512], P('brick', 'frame')
Inputs may be any that keep to these rules, and one draw needn't show every extreme that they name: `block_count`: each frame's counts over the bricks sum to 128, and some pair of the frame holds 8. `pix_index`: the 32 slots of one device (its frames, its brick, padded slots included) include at most 4 slots (counted with repeats, over all of the device's frames) whose pixel block lies in the range 16 * c to 16 * c + 15, for every c; on every device some c has exactly 4 such slots.
All inputs are finite; a program needn't handle non-finite values. No bound on the sum of `block_count` on one device may be relied on, other than what follows from the above.
Results may differ from a plain program's by a relative error of at most 0.00049.
Values may be sent and summed in bfloat16 or wider, within the bound.
A program may use at most 64 MiB of HBM per device.

v0:
```python
import jax
import jax.numpy as jnp
from jax import lax
from jax.sharding import PartitionSpec as P

BLK_DEV = 16


def extended(block, sides, width):
    for axis, dim in sides:
        count = lax.axis_size(axis)
        forward = [(i, i + 1) for i in range(count - 1)]
        backward = [(target, source) for source, target in forward]
        low = lax.ppermute(
            lax.slice_in_dim(block, block.shape[dim] - width, None, axis=dim), axis, forward
        )
        high = lax.ppermute(lax.slice_in_dim(block, 0, width, axis=dim), axis, backward)
        block = jnp.concatenate([low, block, high], axis=dim)
    return block


def on_device(intensity, correction, splitting, block_count, pix_index, vox_offset):
    frames_dev, blocks_per_device, pixel_width = intensity.shape
    max_slots = splitting.shape[2]
    voxels = splitting.shape[4]
    bricks = lax.axis_size("brick")
    groups = lax.axis_size("frame")
    block_rows = BLK_DEV * groups
    slot_count = frames_dev * max_slots
    local_rows = jnp.stack([intensity, correction], axis=2).astype(jnp.bfloat16)
    indices = pix_index.reshape(slot_count)
    frame_slot = jnp.arange(slot_count, dtype=jnp.int32) // max_slots
    gathered = lax.all_gather(local_rows, "brick", axis=1, tiled=True)
    flat_rows = gathered.reshape(frames_dev * blocks_per_device * bricks, 2, pixel_width)
    rows_per_slot = flat_rows[frame_slot * (blocks_per_device * bricks) + indices]
    divided_blocks = splitting.reshape(slot_count, pixel_width, voxels)
    contrib = jnp.einsum(
        "edb,eba->eda", rows_per_slot, divided_blocks, preferred_element_type=jnp.float32
    )
    flat_contrib = contrib.reshape(slot_count, 2 * voxels)
    live_slots = (jnp.arange(max_slots, dtype=jnp.int32)[None, :] < block_count).reshape(slot_count)
    offsets = vox_offset.reshape(slot_count)
    edge_ids = jnp.array([0, block_rows + 1], dtype=jnp.int32)[:, None]
    edge_place = ((offsets[None, :] == edge_ids) & live_slots[None, :]).astype(jnp.float32)
    overhang = jnp.dot(
        edge_place,
        flat_contrib,
        precision=lax.Precision.HIGHEST,
        preferred_element_type=jnp.float32,
    ).reshape(2, 2, voxels)
    neighbours = extended(overhang, (("brick", 0),), 1)
    lower_add = neighbours[0]
    upper_increment = neighbours[3]
    row_ids = jnp.arange(1, block_rows + 1, dtype=jnp.int32)[:, None]
    placement = ((offsets[None, :] == row_ids) & live_slots[None, :]).astype(jnp.float32)
    interior = jnp.dot(
        placement, flat_contrib, precision=lax.Precision.HIGHEST, preferred_element_type=jnp.float32
    )
    interior = interior.reshape(block_rows, 2, voxels)
    interior = interior.at[0].add(lower_add).at[block_rows - 1].add(upper_increment)
    reduced = lax.psum_scatter(interior, "frame", scatter_dimension=0, tiled=True)
    weight = reduced[:, 1]
    merged = reduced[:, 0] / jnp.maximum(weight, 1.0)
    return (merged[None], weight[None])


def solution(mesh):
    placed = (
        P("frame", "brick", None),
        P("frame", "brick", None),
        P("frame", "brick", None, None, None),
        P("frame", "brick"),
        P("frame", "brick", None),
        P("frame", "brick", None),
    )
    return jax.shard_map(
        on_device,
        mesh=mesh,
        in_specs=placed,
        out_specs=(P("brick", "frame", None), P("brick", "frame", None)),
        check_vma=False,
    )
```

profile of v0, /device:TPU:8, one launch (start us, length us, event | category | flops | bytes accessed | tf_op | source)
XLA Modules:
  0.0 130.7 jit_solution(8027460333084453383)
XLA Ops:
  7.2 0.8 convert_bitcast_fusion
  8.0 0.6 pad_maximum_fusion
  8.6 0.0 reduce-scatter.2.cloned.1.call-start
  8.7 0.5 broadcast.132
  9.2 1.3 %reduce.10 = s32[4,8]{1,0:T(4,128)S(1)} reduce(s32[4,1,8]{2,1,0:T(1,128)} %param.15, s32[]{:T(128)} %broadcast.132), dimensions={1}, to_apply=%param.15.reduce_sub_computation.3 | reduce | bytes 260 | tf_op args[4]
  10.5 0.1 reshape.176
  10.6 1.3 %reduce.11 = s32[4,8]{1,0:T(4,128)S(1)} reduce(s32[4,1,8]{2,1,0:T(1,128)} %param.16, s32[]{:T(128)} %broadcast.132), dimensions={1}, to_apply=%param.16.reduce_sub_computation.3 | reduce | bytes 260 | tf_op args[5]
  12.0 0.1 eq.28
  12.1 0.7 iota_compare_fusion
  12.8 0.1 lt.37
  12.9 51.9 %all-gather.2.cloned.1.call-done = bf16[4,512,2,128]{3,1,0,2:T(8,128)(2,1)} async-done(((bf16[4,16,2,128]{3,1,0,2:T(8,128)(2,1)}), bf16[4,512,2,128]{3,1,0,2:T(8,128)(2,1)}) %all-gather.2.cloned.1.call-update) | async-done | bytes 1048592 | tf_op jit(solution)/shard_map/all_gather | solution.py:33
  64.8 2.3 %copy.9 = bf16[4,512,2,128]{3,2,1,0:T(2,128)(2,1)S(1)} copy(bf16[4,512,2,128]{3,1,0,2:T(8,128)(2,1)} %all-gather.2.cloned.1.call-done) | data formatting | bytes 2097152 | tf_op jit(solution)/shard_map/all_gather | solution.py:33
  67.1 0.6 gather_fusion
  67.7 2.8 %fusion.20 = f32[32,2,512]{2,1,0:T(2,128)S(1)} fusion(bf16[32,2,128]{2,1,0:T(2,128)(2,1)S(1)} %gather_fusion, bf16[32,128,512]{2,1,0:T(8,128)(2,1)} %bitcast.35), kind=kOutput, calls=%fused_computation.38 | convolution fusion | flops 8388608 | bytes 4341760 | tf_op jit(solution)/shard_map/edb,eba->eda/dot_general | solution.py:37
  70.6 0.2 fusion.10
  70.8 2.1 %collective-permute-start = (f32[1,2,512]{2,0,1:T(1,128)S(1)}, f32[1,2,512]{2,0,1:T(1,128)S(1)}, u32[]{:S(2)}, u32[]{:S(2)}) collective-permute-start(f32[1,2,512]{2,0,1:T(1,128)S(1)} %bitcast.41), channel_id=1, source_target_pairs={{0,1},{1,2},{2,3},{3,4},{4,5},{5,6},{6,7},{7,8},{8,9},{9,10},{10,1... | collective-permute-start | bytes 12296 | tf_op jit(solution)/shard_map/ppermute | solution.py:14
  73.0 0.5 fusion
  73.5 6.4 %collective-permute-start.1 = (f32[1,2,512]{2,0,1:T(1,128)S(1)}, f32[1,2,512]{2,0,1:T(1,128)S(1)}, u32[]{:S(2)}, u32[]{:S(2)}) collective-permute-start(f32[1,2,512]{2,0,1:T(1,128)S(1)} %bitcast.40), channel_id=1, source_target_pairs={{1,0},{2,1},{3,2},{4,3},{5,4},{6,5},{7,6},{8,7},{9,8},{10,9},{11,1... | collective-permute-start | bytes 12296 | tf_op jit(solution)/shard_map/ppermute | solution.py:17
  79.9 0.1 scatter-add.6
  80.0 1.2 collective-permute-done.1
  81.2 0.1 scatter-add.9
  81.3 0.8 copy-done
  82.1 40.4 %reduce-scatter.2.cloned.1.call-done = f32[16,2,512]{2,0,1:T(8,128)} async-done(((f32[128,2,512]{2,0,1:T(8,128)}), f32[16,2,512]{2,0,1:T(8,128)}) %reduce-scatter.2.cloned.1.call-update) | async-done | bytes 65552 | tf_op jit(solution)/shard_map/reduce_scatter | solution.py:61
  122.5 1.4 %fusion.3 = (f32[1,16,512]{2,1,0:T(8,128)}, f32[1,16,512]{2,1,0:T(8,128)}) fusion(f32[16,2,512]{2,0,1:T(8,128)} %reduce-scatter.2.cloned.1.call-done), kind=kLoop, calls=%fused_computation.6 | loop fusion | flops 16384 | bytes 131072 | tf_op jit(solution)/shard_map/div | solution.py:63
  (13 shorter events, 0.2 us)
Async XLA Ops:
  7.2 57.7 %all-gather.2.cloned.1.call-start = ((), (), s32[]{:S(2)}) async-start(), calls=%async_computation.1 | async-start | bytes 1081344 | tf_op jit(solution)/shard_map/all_gather | solution.py:33
  8.6 113.8 %reduce-scatter.2.cloned.1.call-start = ((), (), s32[]{:S(2)}) async-start(), calls=%async_computation.2 | async-start | bytes 589824 | tf_op jit(solution)/shard_map/reduce_scatter | solution.py:61
  70.8 9.1 %collective-permute-start = (f32[1,2,512]{2,0,1:T(1,128)S(1)}, f32[1,2,512]{2,0,1:T(1,128)S(1)}, u32[]{:S(2)}, u32[]{:S(2)}) collective-permute-start(f32[1,2,512]{2,0,1:T(1,128)S(1)} %bitcast.41), channel_id=1, source_target_pairs={{0,1},{1,2},{2,3},{3,4},{4,5},{5,6},{6,7},{7,8},{8,9},{9,10},{10,1... | collective-permute-start | bytes 12296 | tf_op jit(solution)/shard_map/ppermute | solution.py:14
  73.5 7.7 %collective-permute-start.1 = (f32[1,2,512]{2,0,1:T(1,128)S(1)}, f32[1,2,512]{2,0,1:T(1,128)S(1)}, u32[]{:S(2)}, u32[]{:S(2)}) collective-permute-start(f32[1,2,512]{2,0,1:T(1,128)S(1)} %bitcast.40), channel_id=1, source_target_pairs={{1,0},{2,1},{3,2},{4,3},{5,4},{6,5},{7,6},{8,7},{9,8},{10,9},{11,1... | collective-permute-start | bytes 12296 | tf_op jit(solution)/shard_map/ppermute | solution.py:17
  81.3 0.8 copy-start
Sparse Core Ops, SparseCore 0:
  11.0 53.7 all-gather.1
  82.2 40.1 reduce-scatter.1
where the time goes:
time: 131 us
  waiting for transfers between devices  93.5 us (71%)
  between operations  14.1 us (11%)
  starting transfers between devices  8.65 us (7%)
  other arithmetic  6.26 us (5%)
  local copies, waits for them, and re-layouts  4.63 us (4%)
  matrix products  3.52 us (3%)
    all_gather x1, waiting for transfers between devices, on_device(): gathered = lax.all_gather(local_rows, 'brick', axis=1, tiled=True)  51.9 us
    reduce_scatter x1, waiting for transfers between devices, on_device(): lax.psum_scatter(interior, 'frame', scatter_dimension=0, tiled=True)  40.4 us
    ppermute x1, starting transfers between devices, extended(): lax.ppermute(lax.slice_in_dim(block, 0, width, axis=dim), axis, backward)  6.43 us
    dot_general x1, matrix products, on_device(): jnp.einsum('edb,eba->eda', rows_per_slot, divided_blocks, preferred_eleme...  2.83 us
    unnamed x2, other arithmetic  2.69 us
  transfers between devices with their start and end apart: 4, of which 3 were waited for; matrix products, arithmetic and copies ran while one was open for 4% of the time, Pallas kernels for 0%

commit v1 on v0

--- a/solution.py
+++ b/solution.py
@@ -30,7 +30,9 @@
     local_rows = jnp.stack([intensity, correction], axis=2).astype(jnp.bfloat16)
     indices = pix_index.reshape(slot_count)
     frame_slot = jnp.arange(slot_count, dtype=jnp.int32) // max_slots
-    gathered = lax.all_gather(local_rows, "brick", axis=1, tiled=True)
+    gathered = jnp.concatenate(
+        lax.all_to_all(jnp.stack([local_rows] * lax.axis_size("brick")), "brick", 0, 0), axis=1
+    )
     flat_rows = gathered.reshape(frames_dev * blocks_per_device * bricks, 2, pixel_width)
     rows_per_slot = flat_rows[frame_slot * (blocks_per_device * bricks) + indices]
     divided_blocks = splitting.reshape(slot_count, pixel_width, voxels)

time: 131 us -> 122 us (0.931)
  waiting for transfers between devices: 93.5 us -> 65.7 us
  starting transfers between devices: 8.65 us -> 20.3 us
  local copies, waits for them, and re-layouts: 4.63 us -> 12.4 us
    all_gather x1 -> x0, waiting for transfers between devices: 51.9 us -> none  [on_device(): gathered = lax.all_gather(local_rows, 'brick', axis=1, tiled=True)]
    all_to_all x0 -> x1, waiting for transfers between devices: none -> 23.4 us  [on_device(): lax.all_to_all(jnp.stack([local_rows] * lax.axis_size('brick')), 'brick',...]
    all_to_all x0 -> x1, starting transfers between devices: none -> 11.7 us  [on_device(): lax.all_to_all(jnp.stack([local_rows] * lax.axis_size('brick')), 'brick',...]
    another operation x0 -> x2, local copies, waits for them, and re-layouts: none -> 9.91 us  [the longest x1 8.68 us: on_device(): gathered.reshape(frames_dev * blocks_per_device * bricks, 2, pixel_width)]
    all_gather x1 -> x0, local copies, waits for them, and re-layouts: 2.3 us -> none  [on_device(): gathered = lax.all_gather(local_rows, 'brick', axis=1, tiled=True)]
where the time goes in v1:
time: 122 us
  waiting for transfers between devices  65.7 us (54%)
  starting transfers between devices  20.3 us (17%)
  between operations  14.1 us (12%)
  local copies, waits for them, and re-layouts  12.4 us (10%)
  other arithmetic  5.65 us (5%)
  matrix products  3.52 us (3%)
    reduce_scatter x1, waiting for transfers between devices, on_device(): lax.psum_scatter(interior, 'frame', scatter_dimension=0, tiled=True)  41.1 us
    all_to_all x1, waiting for transfers between devices, on_device(): lax.all_to_all(jnp.stack([local_rows] * lax.axis_size('brick')), 'brick',...  23.4 us
    all_to_all x1, starting transfers between devices, on_device(): lax.all_to_all(jnp.stack([local_rows] * lax.axis_size('brick')), 'brick',...  11.7 us
    another operation x1, local copies, waits for them, and re-layouts, on_device(): gathered.reshape(frames_dev * blocks_per_device * bricks, 2, pixel_width)  8.68 us
    ppermute x1, starting transfers between devices, extended(): lax.ppermute(lax.slice_in_dim(block, 0, width, axis=dim), axis, backward)  5.75 us
    dot_general x1, matrix products, on_device(): jnp.einsum('edb,eba->eda', rows_per_slot, divided_blocks, preferred_eleme...  2.83 us
    ppermute x1, starting transfers between devices, extended(): lax.ppermute(lax.slice_in_dim(block, block.shape[dim] - width, None, axis...  2.82 us
    unnamed x2, other arithmetic  2.69 us
  transfers between devices with their start and end apart: 4, of which 3 were waited for; matrix products, arithmetic and copies ran while one was open for 4% of the time, Pallas kernels for 0%

profile of v1, /device:TPU:8, one launch (start us, length us, event | category | flops | bytes accessed | tf_op | source)
XLA Modules:
  0.0 121.7 jit_solution(6521886235784570805)
XLA Ops:
  7.2 0.8 convert_bitcast_fusion
  8.0 1.2 %stack.11 = bf16[32,4,16,2,128]{4,2,1,3,0:T(8,128)(2,1)} broadcast(bf16[4,16,2,128]{3,1,0,2:T(8,128)(2,1)S(1)} %pad_maximum_fusion), dimensions={1,2,3,4} | broadcast | bytes 1081344 | tf_op jit(solution)/shard_map/stack | solution.py:34
  9.2 11.7 %all-to-all-start = ((bf16[32,4,16,2,128]{4,2,1,3,0:T(8,128)(2,1)}), bf16[32,4,16,2,128]{4,2,1,3,0:T(8,128)(2,1)S(1)}, u32[]{:S(2)}, u32[]{:S(2)}) async-start(bf16[32,4,16,2,128]{4,2,1,3,0:T(8,128)(2,1)} %stack.11), calls=%async_computation | async-start | bytes 2097152 | tf_op jit(solution)/shard_map/all_to_all | solution.py:34
  20.9 0.5 broadcast.133
  21.5 1.3 %reduce.10 = s32[4,8]{1,0:T(4,128)S(1)} reduce(s32[4,1,8]{2,1,0:T(1,128)} %param.15, s32[]{:T(128)} %broadcast.133), dimensions={1}, to_apply=%param.15.reduce_sub_computation.3 | reduce | bytes 260 | tf_op args[4]
  22.8 0.1 reshape.187
  22.9 1.3 %reduce.11 = s32[4,8]{1,0:T(4,128)S(1)} reduce(s32[4,1,8]{2,1,0:T(1,128)} %param.16, s32[]{:T(128)} %broadcast.133), dimensions={1}, to_apply=%param.16.reduce_sub_computation.3 | reduce | bytes 260 | tf_op args[5]
  24.2 0.1 eq.28
  24.3 0.7 iota_compare_fusion
  25.1 0.1 lt.37
  25.2 23.4 %all-to-all-done = bf16[32,4,16,2,128]{4,2,1,3,0:T(8,128)(2,1)S(1)} async-done(((bf16[32,4,16,2,128]{4,2,1,3,0:T(8,128)(2,1)}), bf16[32,4,16,2,128]{4,2,1,3,0:T(8,128)(2,1)S(1)}, u32[]{:S(2)}, u32[]{:S(2)}) %all-to-all-start) | async-done | bytes 1048608 | tf_op jit(solution)/shard_map/all_to_all | solution.py:34
  48.6 0.2 copy.14
  48.8 8.7 %copy.15 = bf16[2048,2,128]{2,1,0:T(2,128)(2,1)S(1)} copy(bf16[2048,2,128]{2,0,1:T(8,128)(2,1)S(1)} %bitcast.38) | data formatting | bytes 2097152 | tf_op jit(solution)/shard_map/reshape;reshape | solution.py:36
  57.4 0.6 gather_fusion
  58.0 2.8 %fusion.20 = f32[32,2,512]{2,1,0:T(2,128)S(1)} fusion(bf16[32,2,128]{2,1,0:T(2,128)(2,1)S(1)} %gather_fusion, bf16[32,128,512]{2,1,0:T(8,128)(2,1)} %bitcast.37), kind=kOutput, calls=%fused_computation.38 | convolution fusion | flops 8388608 | bytes 4341760 | tf_op jit(solution)/shard_map/edb,eba->eda/dot_general | solution.py:39
  60.9 0.2 fusion.10
  61.1 2.8 %collective-permute-start = (f32[1,2,512]{2,0,1:T(1,128)S(1)}, f32[1,2,512]{2,0,1:T(1,128)S(1)}, u32[]{:S(2)}, u32[]{:S(2)}) collective-permute-start(f32[1,2,512]{2,0,1:T(1,128)S(1)} %bitcast.43), channel_id=1, source_target_pairs={{0,1},{1,2},{2,3},{3,4},{4,5},{5,6},{6,7},{7,8},{8,9},{9,10},{10,1... | collective-permute-start | bytes 12296 | tf_op jit(solution)/shard_map/ppermute | solution.py:14
  64.0 0.5 fusion
  64.5 5.8 %collective-permute-start.1 = (f32[1,2,512]{2,0,1:T(1,128)S(1)}, f32[1,2,512]{2,0,1:T(1,128)S(1)}, u32[]{:S(2)}, u32[]{:S(2)}) collective-permute-start(f32[1,2,512]{2,0,1:T(1,128)S(1)} %bitcast.42), channel_id=1, source_target_pairs={{1,0},{2,1},{3,2},{4,3},{5,4},{6,5},{7,6},{8,7},{9,8},{10,9},{11,1... | collective-permute-start | bytes 12296 | tf_op jit(solution)/shard_map/ppermute | solution.py:17
  70.2 0.1 scatter-add.6
  70.3 1.2 collective-permute-done.1
  71.6 0.8 copy-done
  72.4 41.1 %reduce-scatter.2.cloned.1.call-done = f32[16,2,512]{2,0,1:T(8,128)} async-done(((f32[128,2,512]{2,0,1:T(8,128)}), f32[16,2,512]{2,0,1:T(8,128)}) %reduce-scatter.2.cloned.1.call-update) | async-done | bytes 65552 | tf_op jit(solution)/shard_map/reduce_scatter | solution.py:63
  113.5 1.4 %fusion.3 = (f32[1,16,512]{2,1,0:T(8,128)}, f32[1,16,512]{2,1,0:T(8,128)}) fusion(f32[16,2,512]{2,0,1:T(8,128)} %reduce-scatter.2.cloned.1.call-done), kind=kLoop, calls=%fused_computation.6 | loop fusion | flops 16384 | bytes 131072 | tf_op jit(solution)/shard_map/div | solution.py:65
  (14 shorter events, 0.2 us)
Async XLA Ops:
  9.2 39.4 %all-to-all-start = ((bf16[32,4,16,2,128]{4,2,1,3,0:T(8,128)(2,1)}), bf16[32,4,16,2,128]{4,2,1,3,0:T(8,128)(2,1)S(1)}, u32[]{:S(2)}, u32[]{:S(2)}) async-start(bf16[32,4,16,2,128]{4,2,1,3,0:T(8,128)(2,1)} %stack.11), calls=%async_computation | async-start | bytes 2097152 | tf_op jit(solution)/shard_map/all_to_all | solution.py:34
  20.9 92.6 %reduce-scatter.2.cloned.1.call-start = ((), (), s32[]{:S(2)}) async-start(), calls=%async_computation.2 | async-start | bytes 589824 | tf_op jit(solution)/shard_map/reduce_scatter | solution.py:63
  61.1 9.1 %collective-permute-start = (f32[1,2,512]{2,0,1:T(1,128)S(1)}, f32[1,2,512]{2,0,1:T(1,128)S(1)}, u32[]{:S(2)}, u32[]{:S(2)}) collective-permute-start(f32[1,2,512]{2,0,1:T(1,128)S(1)} %bitcast.43), channel_id=1, source_target_pairs={{0,1},{1,2},{2,3},{3,4},{4,5},{5,6},{6,7},{7,8},{8,9},{9,10},{10,1... | collective-permute-start | bytes 12296 | tf_op jit(solution)/shard_map/ppermute | solution.py:14
  64.5 7.1 %collective-permute-start.1 = (f32[1,2,512]{2,0,1:T(1,128)S(1)}, f32[1,2,512]{2,0,1:T(1,128)S(1)}, u32[]{:S(2)}, u32[]{:S(2)}) collective-permute-start(f32[1,2,512]{2,0,1:T(1,128)S(1)} %bitcast.42), channel_id=1, source_target_pairs={{1,0},{2,1},{3,2},{4,3},{5,4},{6,5},{7,6},{8,7},{9,8},{10,9},{11,1... | collective-permute-start | bytes 12296 | tf_op jit(solution)/shard_map/ppermute | solution.py:17
  71.6 0.8 copy-start
Sparse Core Ops, SparseCore 0:
  72.5 40.8 reduce-scatter.1
